TPU v7x, 32 devices: a whole 2x2x4 slice. The times are simulated.
32 devices in a mesh: gx: 4 (over z), gy: 8 (over y, x, core).
Axes of the slice: x: 2, y: 2, z: 4, core: 2. Of those that a mesh axis runs over, the one named last changes fastest.
Arguments:
- heat_source: float32 [1536, 1024], P(('gx', 'gy')), may hold values from -18 to 18
- stiffness: float32 [512, 384, 384], P(('gx', 'gy')), may hold values from -1 to 32, as said below
- element_faces: int32 [512, 6], P(('gx', 'gy')), may hold values from 0 to 1535, as said below
Outputs:
- solution: float32 [1536, 1024], P(('gx', 'gy'))
- residual: float32 [1536, 1024], P(('gx', 'gy'))
Inputs may be any that keep to these rules, and one draw needn't show every extreme that they name: `element_faces`: the elements form a periodic grid of 8 x 16 x 4 hexahedra; device (i, j) of gx and gy holds the block of 2 x 2 x 4 elements at streamwise block i and spanwise block j, in a local order of its own, and owns the lower x, lower y and lower z faces of its elements, numbered in an order of its own. So every face number appears exactly twice, and a device's elements reference faces of itself, of the next device along gx (cyclic, same gy index; exactly 8 references) and of the next device along gy (cyclic, same gx index; exactly 8 references). `stiffness`: each element matrix is symmetric with a positive diagonal and strictly diagonally dominant.
All inputs are finite; a program needn't handle non-finite values.
Results may differ from a plain program's by a relative error of at most 0.0002.
Values sent between devices are 32-bit elements; how exact they have to be, the bound alone decides.
A program may use at most 128 MiB of HBM per device.

v0:
```python
import jax
import jax.numpy as jnp
from jax import lax
from jax.sharding import PartitionSpec as P

BLOCK = 64
EX = 2
EY = 2
EZ = 4
SOURCES = 16
ITERS = 3


def passed_along(value, axis, steps):
    count = lax.axis_size(axis)
    pairs = [(source, (source + steps) % count) for source in range(count)]
    return lax.ppermute(value, axis, pairs)


def source_sum(first_vec, second_vec):
    return jnp.sum(
        (first_vec * second_vec).reshape(first_vec.shape[0], SOURCES, BLOCK), axis=(0, 2)
    )


def spread(per_source):
    return jnp.repeat(per_source, BLOCK)[None, :]


def local(heat_source, stiffness, element_faces):
    face_dev = heat_source.shape[0]
    elements = element_faces.shape[0]
    references = 6 * elements
    row_width = heat_source.shape[1]
    outer = lax.axis_size("gx")
    inner = lax.axis_size("gy")
    outer_at = lax.axis_index("gx")
    inner_at = lax.axis_index("gy")
    self_dev = outer_at * inner + inner_at
    x_next = (outer_at + 1) % outer * inner + inner_at
    y_next = outer_at * inner + (inner_at + 1) % inner
    x_count = EY * EZ
    y_count = EX * EZ
    flat_faces = element_faces.reshape(references)
    owner_dev = flat_faces // face_dev
    local_face = flat_faces % face_dev
    is_self = owner_dev == self_dev
    is_x = owner_dev == x_next
    is_y = owner_dev == y_next
    rank_x = jnp.cumsum(is_x.astype(jnp.int32)) - 1
    rank_y = jnp.cumsum(is_y.astype(jnp.int32)) - 1
    ref_ids = jnp.arange(references, dtype=jnp.int32)
    refs_x = (
        jnp.zeros((x_count,), jnp.int32)
        .at[jnp.where(is_x, rank_x, x_count)]
        .set(ref_ids, mode="drop")
    )
    refs_y = (
        jnp.zeros((y_count,), jnp.int32)
        .at[jnp.where(is_y, rank_y, y_count)]
        .set(ref_ids, mode="drop")
    )
    wanted_x = passed_along(local_face[refs_x], "gx", 1)
    wanted_y = passed_along(local_face[refs_y], "gy", 1)
    table_index = jnp.where(
        is_self, local_face, jnp.where(is_x, face_dev + rank_x, face_dev + x_count + rank_y)
    )
    self_target = jnp.where(is_self, local_face, face_dev)
    matrix = stiffness.reshape(elements, 6, BLOCK, 6, BLOCK)

    def send_traces(rows_x, rows_y):
        got_x = passed_along(rows_x, "gx", -1)
        got_y = passed_along(rows_y, "gy", -1)
        return (got_x, got_y)

    def return_fluxes(rows_x, rows_y):
        got_x = passed_along(rows_x, "gx", 1)
        got_y = passed_along(rows_y, "gy", 1)
        return (got_x, got_y)

    def operate(vector):
        incoming_x, incoming_y = send_traces(vector[wanted_x], vector[wanted_y])
        table = jnp.concatenate([vector, incoming_x, incoming_y], axis=0)
        blocks = table[table_index].reshape(elements, 6, SOURCES, BLOCK)
        flux_terms = jnp.einsum(
            "ekbjc,ejsc->eksb",
            matrix,
            blocks,
            precision=lax.Precision.HIGHEST,
            preferred_element_type=jnp.float32,
        )
        flux_rows = flux_terms.reshape(references, row_width)
        back_x, back_y = return_fluxes(flux_rows[refs_x], flux_rows[refs_y])
        result = (
            jnp.zeros((face_dev + 1, row_width), jnp.float32)
            .at[self_target]
            .add(flux_rows)[:face_dev]
        )
        return result.at[wanted_x].add(back_x).at[wanted_y].add(back_y)

    def pair_sums(residual, applied):
        return lax.psum(
            (source_sum(residual, residual), source_sum(residual, applied)), ("gx", "gy")
        )

    solution = jnp.zeros_like(heat_source)
    residual = heat_source
    applied = operate(residual)
    norm_now, product = pair_sums(residual, applied)
    step_size = norm_now / product
    direction = residual
    applied_dir = applied
    for iteration in range(ITERS):
        solution = solution + spread(step_size) * direction
        residual = residual - spread(step_size) * applied_dir
        if iteration + 1 < ITERS:
            applied = operate(residual)
            norm_next, product = pair_sums(residual, applied)
            beta_ratio = norm_next / norm_now
            step_size = norm_next / (product - beta_ratio * norm_next / step_size)
            direction = residual + spread(beta_ratio) * direction
            applied_dir = applied + spread(beta_ratio) * applied_dir
            norm_now = norm_next
    return (solution, residual)


def solution(mesh):
    return jax.shard_map(
        local,
        mesh=mesh,
        in_specs=(P(("gx", "gy"), None), P(("gx", "gy"), None, None), P(("gx", "gy"), None)),
        out_specs=(P(("gx", "gy"), None), P(("gx", "gy"), None)),
        check_vma=False,
    )
```

profile of v0, /device:TPU:0, one launch (start us, length us, event | category | flops | bytes accessed | tf_op | source)
XLA Modules:
  0.0 282.2 jit_solution(6366592186655513015)
XLA Ops:
  6.9 2.6 collective-permute-start
  9.5 3.6 %collective-permute-done = s32[8]{0:T(128)S(1)} collective-permute-done((s32[8]{0:T(128)S(1)}, s32[8]{0:T(128)S(1)}, u32[]{:S(2)}, u32[]{:S(2)}) %collective-permute-start) | collective-permute-done | bytes 64 | tf_op jit(solution)/shard_map/ppermute | solution.py:17
  13.1 1.5 gather_fusion.1
  14.6 1.5 gather_fusion.3
  16.1 1.8 collective-permute-start.3
  17.9 1.7 collective-permute-start.1
  19.7 17.1 %reshape.252 = f32[16,6,64,6,64]{4,3,2,1,0:T(8,128)} reshape(f32[16,384,384]{2,1,0:T(8,128)} %param.4) | data formatting | bytes 18874368 | tf_op jit(solution)/shard_map/reshape | solution.py:69
  37.8 28.8 %fusion.6 = f32[16,6,16,64]{3,2,1,0:T(8,128)S(1)} fusion(f32[16,6,64,6,64]{4,3,2,1,0:T(8,128)} %reshape.252, f32[16,6,16,64,1]{3,2,1,0,4:T(8,128)S(1)} %reshape.502), kind=kOutput, calls=%fused_computation.34 | convolution fusion | flops 452984832 | bytes 10223616 | tf_op jit(solution)/shard_map/ekbjc,ejsc->eksb/dot_general | solution.py:85
  68.4 1.4 scatter_custom_fusion.2
  69.8 3.4 %collective-permute-done.4 = f32[8,1024]{1,0:T(8,128)S(1)} collective-permute-done((f32[8,1024]{1,0:T(8,128)S(1)}, f32[8,1024]{1,0:T(8,128)S(1)}, u32[]{:S(2)}, u32[]{:S(2)}) %collective-permute-start.4) | collective-permute-done | bytes 32800 | tf_op jit(solution)/shard_map/ppermute | solution.py:17
  75.2 37.6 %all-reduce.2 = (f32[16]{0:T(128)S(1)}, f32[16]{0:T(128)S(1)}) all-reduce(f32[16]{0:T(128)S(1)} %reduce_sum.74, f32[16]{0:T(128)S(1)} %reduce_sum.77), channel_id=1, replica_groups=mesh['gx'=4,'gy'=8] {'gx','gy'}, use_global_device_ids=true, to_apply=%region_2.3 | all-reduce | flops 32 | bytes 256 | tf_op jit(solution)/shard_map/psum | solution.py:102
  114.1 1.7 collective-permute-start.6
  116.4 1.8 collective-permute-done.6
  119.2 28.8 %fusion.9 = f32[16,6,16,64]{3,2,1,0:T(8,128)S(1)} fusion(f32[16,6,64,6,64]{4,3,2,1,0:T(8,128)} %reshape.252, f32[16,6,16,64,1]{3,2,1,0,4:T(8,128)S(1)} %reshape.504), kind=kOutput, calls=%fused_computation.35 | convolution fusion | flops 452984832 | bytes 10223616 | tf_op jit(solution)/shard_map/ekbjc,ejsc->eksb/dot_general | solution.py:85
  148.9 2.1 collective-permute-start.8
  151.6 1.4 scatter_custom_fusion.5
  153.0 1.6 collective-permute-done.8
  157.0 39.8 %all-reduce.1 = (f32[16]{0:T(128)S(1)}, f32[16]{0:T(128)S(1)}) all-reduce(f32[16]{0:T(128)S(1)} %reduce_sum.83, f32[16]{0:T(128)S(1)} %reduce_sum.89), channel_id=1, replica_groups=mesh['gx'=4,'gy'=8] {'gx','gy'}, use_global_device_ids=true, to_apply=%region_15.16 | all-reduce | flops 32 | bytes 256 | tf_op jit(solution)/shard_map/psum | solution.py:102
  198.3 2.0 collective-permute-start.10
  200.9 1.3 collective-permute-done.10
  203.5 28.8 %fusion.12 = f32[16,6,16,64]{3,2,1,0:T(8,128)S(1)} fusion(f32[16,6,64,6,64]{4,3,2,1,0:T(8,128)} %reshape.252, f32[16,6,16,64,1]{3,2,1,0,4:T(8,128)S(1)} %reshape.506), kind=kOutput, calls=%fused_computation.36 | convolution fusion | flops 452984832 | bytes 10223616 | tf_op jit(solution)/shard_map/ekbjc,ejsc->eksb/dot_general | solution.py:85
  235.6 1.4 scatter_custom_fusion.8
  237.0 1.9 collective-permute-done.12
  240.9 40.1 %all-reduce = (f32[16]{0:T(128)S(1)}, f32[16]{0:T(128)S(1)}) all-reduce(f32[16]{0:T(128)S(1)} %reduce_sum.110, f32[16]{0:T(128)S(1)} %reduce_sum.113), channel_id=1, replica_groups=mesh['gx'=4,'gy'=8] {'gx','gy'}, use_global_device_ids=true, to_apply=%region_24.25 | all-reduce | flops 32 | bytes 256 | tf_op jit(solution)/shard_map/psum | solution.py:102
  (109 shorter events, 27.3 us)
Async XLA Ops:
  0.6 36.2 %copy-start = (f32[48,1024]{1,0:T(8,128)S(1)}, f32[48,1024]{1,0:T(8,128)}, u32[]{:S(2)}) copy-start(f32[48,1024]{1,0:T(8,128)} %param.3) | copy-start | bytes 589828
  4.8 4.7 %collective-permute-start.2 = (s32[8]{0:T(128)S(1)}, s32[8]{0:T(128)S(1)}, u32[]{:S(2)}, u32[]{:S(2)}) collective-permute-start(s32[8]{0:T(128)S(1)} %gather_fusion.2), channel_id=1, source_target_pairs={{0,1},{1,2},{2,3},{3,4},{4,5},{5,6},{6,7},{7,0},{8,9},{9,10},{10,1... | collective-permute-start | bytes 104 | tf_op jit(solution)/shard_map/ppermute | solution.py:17
  6.9 6.2 %collective-permute-start = (s32[8]{0:T(128)S(1)}, s32[8]{0:T(128)S(1)}, u32[]{:S(2)}, u32[]{:S(2)}) collective-permute-start(s32[8]{0:T(128)S(1)} %gather_fusion), channel_id=1, source_target_pairs={{0,8},{8,16},{16,24},{24,0},{1,9},{9,17},{17,25},{25,1},{2,10},{10... | collective-permute-start | bytes 104 | tf_op jit(solution)/shard_map/ppermute | solution.py:17
  16.1 20.7 %collective-permute-start.3 = (f32[8,1024]{1,0:T(8,128)S(1)}, f32[8,1024]{1,0:T(8,128)S(1)}, u32[]{:S(2)}, u32[]{:S(2)}) collective-permute-start(f32[8,1024]{1,0:T(8,128)S(1)} %gather_fusion.3), channel_id=1, source_target_pairs={{0,7},{1,0},{2,1},{3,2},{4,3},{5,4},{6,5},{7,6},{8,15},{9,8},{10,9... | collective-permute-start | bytes 98312 | tf_op jit(solution)/shard_map/ppermute | solution.py:17
  17.9 18.9 %collective-permute-start.1 = (f32[8,1024]{1,0:T(8,128)S(1)}, f32[8,1024]{1,0:T(8,128)S(1)}, u32[]{:S(2)}, u32[]{:S(2)}) collective-permute-start(f32[8,1024]{1,0:T(8,128)S(1)} %gather_fusion.1), channel_id=1, source_target_pairs={{0,24},{8,0},{16,8},{24,16},{1,25},{9,1},{17,9},{25,17},{2,26},{10... | collective-permute-start | bytes 98312 | tf_op jit(solution)/shard_map/ppermute | solution.py:17
  67.4 5.8 %collective-permute-start.4 = (f32[8,1024]{1,0:T(8,128)S(1)}, f32[8,1024]{1,0:T(8,128)S(1)}, u32[]{:S(2)}, u32[]{:S(2)}) collective-permute-start(f32[8,1024]{1,0:T(8,128)S(1)} %gather_fusion.5), channel_id=1, source_target_pairs={{0,8},{8,16},{16,24},{24,0},{1,9},{9,17},{17,25},{25,1},{2,10},{10... | collective-permute-start | bytes 98312 | tf_op jit(solution)/shard_map/ppermute | solution.py:17
  68.3 5.6 %collective-permute-start.5 = (f32[8,1024]{1,0:T(8,128)S(1)}, f32[8,1024]{1,0:T(8,128)S(1)}, u32[]{:S(2)}, u32[]{:S(2)}) collective-permute-start(f32[8,1024]{1,0:T(8,128)S(1)} %gather_fusion.6), channel_id=1, source_target_pairs={{0,1},{1,2},{2,3},{3,4},{4,5},{5,6},{6,7},{7,0},{8,9},{9,10},{10,1... | collective-permute-start | bytes 98312 | tf_op jit(solution)/shard_map/ppermute | solution.py:17
  114.1 4.2 %collective-permute-start.6 = (f32[8,1024]{1,0:T(8,128)S(1)}, f32[8,1024]{1,0:T(8,128)S(1)}, u32[]{:S(2)}, u32[]{:S(2)}) collective-permute-start(f32[8,1024]{1,0:T(8,128)S(1)} %gather_fusion.7), channel_id=1, source_target_pairs={{0,24},{8,0},{16,8},{24,16},{1,25},{9,1},{17,9},{25,17},{2,26},{10... | collective-permute-start | bytes 98312 | tf_op jit(solution)/shard_map/ppermute | solution.py:17
  115.8 2.5 collective-permute-start.7
  148.9 5.8 %collective-permute-start.8 = (f32[8,1024]{1,0:T(8,128)S(1)}, f32[8,1024]{1,0:T(8,128)S(1)}, u32[]{:S(2)}, u32[]{:S(2)}) collective-permute-start(f32[8,1024]{1,0:T(8,128)S(1)} %gather_fusion.10), channel_id=1, source_target_pairs={{0,8},{8,16},{16,24},{24,0},{1,9},{9,17},{17,25},{25,1},{2,10},{10... | collective-permute-start | bytes 98312 | tf_op jit(solution)/shard_map/ppermute | solution.py:17
  151.5 4.3 %collective-permute-start.9 = (f32[8,1024]{1,0:T(8,128)S(1)}, f32[8,1024]{1,0:T(8,128)S(1)}, u32[]{:S(2)}, u32[]{:S(2)}) collective-permute-start(f32[8,1024]{1,0:T(8,128)S(1)} %gather_fusion.11), channel_id=1, source_target_pairs={{0,1},{1,2},{2,3},{3,4},{4,5},{5,6},{6,7},{7,0},{8,9},{9,10},{10,1... | collective-permute-start | bytes 98312 | tf_op jit(solution)/shard_map/ppermute | solution.py:17
  198.3 4.0 %collective-permute-start.10 = (f32[8,1024]{1,0:T(8,128)S(1)}, f32[8,1024]{1,0:T(8,128)S(1)}, u32[]{:S(2)}, u32[]{:S(2)}) collective-permute-start(f32[8,1024]{1,0:T(8,128)S(1)} %gather_fusion.12), channel_id=1, source_target_pairs={{0,24},{8,0},{16,8},{24,16},{1,25},{9,1},{17,9},{25,17},{2,26},{10... | collective-permute-start | bytes 98312 | tf_op jit(solution)/shard_map/ppermute | solution.py:17
  200.3 2.2 collective-permute-start.11
  233.1 5.8 %collective-permute-start.12 = (f32[8,1024]{1,0:T(8,128)S(1)}, f32[8,1024]{1,0:T(8,128)S(1)}, u32[]{:S(2)}, u32[]{:S(2)}) collective-permute-start(f32[8,1024]{1,0:T(8,128)S(1)} %gather_fusion.15), channel_id=1, source_target_pairs={{0,8},{8,16},{16,24},{24,0},{1,9},{9,17},{17,25},{25,1},{2,10},{10... | collective-permute-start | bytes 98312 | tf_op jit(solution)/shard_map/ppermute | solution.py:17
  234.7 4.9 %collective-permute-start.13 = (f32[8,1024]{1,0:T(8,128)S(1)}, f32[8,1024]{1,0:T(8,128)S(1)}, u32[]{:S(2)}, u32[]{:S(2)}) collective-permute-start(f32[8,1024]{1,0:T(8,128)S(1)} %gather_fusion.16), channel_id=1, source_target_pairs={{0,1},{1,2},{2,3},{3,4},{4,5},{5,6},{6,7},{7,0},{8,9},{9,10},{10,1... | collective-permute-start | bytes 98312 | tf_op jit(solution)/shard_map/ppermute | solution.py:17
where the time goes:
time: 283 us; the launch traced here: 282 us
  blocking collectives  117 us (41%)
  matrix products  86.4 us (31%)
  local copies, waits for them, and re-layouts  34.2 us (12%)
  starting transfers between devices  16.1 us (6%)
  waiting for transfers between devices  14.2 us (5%)
  other arithmetic  12.6 us (4%)
    psum x3, blocking collectives, pair_sums(): lax.psum((source_sum(residual, residual), source_sum(residual, applied)),...  117 us
    dot_general x3, matrix products, operate(): jnp.einsum('ekbjc,ejsc->eksb', matrix, blocks, precision=lax.Precision.HI...  86.4 us
    reshape x1, local copies, waits for them, and re-layouts, local(): matrix = stiffness.reshape(elements, 6, BLOCK, 6, BLOCK)  17.1 us
    ppermute x14, starting transfers between devices, passed_along(): return lax.ppermute(value, axis, pairs)  16.1 us
    ppermute x14, waiting for transfers between devices, passed_along(): return lax.ppermute(value, axis, pairs)  14.2 us
  transfers between devices with their start and end apart: 14, of which 8 were waited for; matrix products, arithmetic and copies ran while one was open for 10% of the time, Pallas kernels for 0%

commit v1 on v0

v1 whole, which is shorter than its diff:
```python
import jax
import jax.numpy as jnp
from jax import lax
from jax.experimental import pallas as pl
from jax.experimental.pallas import tpu as pltpu
from jax.sharding import PartitionSpec as P

BLOCK = 64
EX = 2
EY = 2
EZ = 4
HALF = BLOCK
LANES = 2 * BLOCK
F32 = jnp.float32
BF16 = jnp.bfloat16
MESH = pl.DeviceIdType.MESH
UNROLL = 2


def index_tables(faces, base, count, face_dev, nx, ny, idx):
    sub = lax.broadcasted_iota(jnp.int32, (count, count), 0)
    lane = lax.broadcasted_iota(jnp.int32, (count, count), 1)
    eye = sub == lane
    slots = 6 * count
    cols = [faces[:, k : k + 1] for k in range(6)]
    rows = [jnp.sum(jnp.where(eye, c, 0), axis=0, keepdims=True) for c in cols]
    idx[...] = jnp.zeros(idx.shape, jnp.int32)
    sizes = [nx, nx, ny, ny]
    starts = [slots, slots + nx, slots + 2 * nx, slots + 2 * nx + ny]
    for axis in range(3):
        low, up = 2 * axis, 2 * axis + 1
        for k, other in ((low, up), (up, low)):
            match = (cols[other] == rows[k]).astype(jnp.int32)
            has = jnp.sum(match, axis=0, keepdims=True)
            place = jnp.sum(match * (other * count + sub), axis=0, keepdims=True)
            local = rows[k] - base
            if axis == 2:
                idx[k : k + 1, 0:count] = place
                idx[6 + k : 7 + k, 0:count] = local
                continue
            match_c = (cols[k] == rows[other]).astype(jnp.int32)
            has_c = jnp.sum(match_c, axis=1, keepdims=True)
            before = jnp.where((has_c == 0) & (cols[k] < rows[k]), 1, 0)
            rank = jnp.sum(before, axis=0, keepdims=True)
            before_c = jnp.where((has == 0) & (rows[k] < cols[k]), 1, 0)
            rank_c = jnp.sum(before_c, axis=1, keepdims=True)
            chosen = (has_c == 0) & (rank_c == lane)
            listed = jnp.sum(jnp.where(chosen, k * count + sub, 0), axis=0, keepdims=True)
            idx[k : k + 1, 0:count] = jnp.where(has > 0, place, starts[k] + rank)
            if k == low:
                traces = jnp.where(chosen, cols[k] - base, 0)
                idx[17 + axis : 18 + axis, 0:count] = jnp.sum(traces, axis=0, keepdims=True)
                idx[6 + k : 7 + k, 0:count] = local
            else:
                first = face_dev + (0 if axis == 0 else nx)
                idx[6 + k : 7 + k, 0:count] = jnp.where(has > 0, local, first + rank)
            idx[12 + k : 13 + k, 0:count] = listed
    wide = lax.broadcasted_iota(jnp.int32, (count, LANES), 1)
    wide_sub = lax.broadcasted_iota(jnp.int32, (count, LANES), 0)
    inverse = jnp.zeros((1, LANES), jnp.int32)
    for k in (0, 2, 4):
        owned = (cols[k] - base) == wide
        inverse = inverse + jnp.sum(
            jnp.where(owned, k * count + wide_sub, 0), axis=0, keepdims=True
        )
    idx[16:17, :] = inverse
    idx[0:6, :] = jnp.clip(idx[0:6, :], 0, slots + 2 * (nx + ny) - 1)
    idx[6:12, :] = jnp.clip(idx[6:12, :], 0, face_dev + nx + ny - 1)
    idx[12:17, :] = jnp.clip(idx[12:17, :], 0, slots - 1)
    idx[17:19, :] = jnp.clip(idx[17:19, :], 0, face_dev - 1)


def make_kernel(outer, inner, count, face_dev, groups, nx, ny):
    slots = 6 * count
    lows = (0, 2, 4)

    def kernel(heat_ref, faces_ref, stiff_ref, sol_ref, res_ref,
               raw, high, low, tile_rows, table, v0, v1, v2, flux, q1,
               idx_v, idx, send0, recv0, sends, recvs, txs, rxx, rxy, txy,
               raw_sem, idx_sem, s0_sem, r0_sem, ss_sem, rr_sem,
               xs_sem, xr_sem, ys_sem, yr_sem):
        gx = lax.axis_index("gx")
        gy = lax.axis_index("gy")
        x_next = (lax.rem(gx + 1, outer), gy)
        x_prev = (lax.rem(gx + outer - 1, outer), gy)
        y_next = (gx, lax.rem(gy + 1, inner))
        y_prev = (gx, lax.rem(gy + inner - 1, inner))

        def raw_copy(e):
            return pltpu.make_async_copy(stiff_ref.at[e], raw.at[e], raw_sem.at[e])

        for e in range(count):
            raw_copy(e).start()
        barrier = pltpu.get_barrier_semaphore()
        for d in range(1, outer):
            pl.semaphore_signal(barrier, inc=1, device_id=(lax.rem(gx + d, outer), gy),
                                device_id_type=MESH)
        for d in range(1, inner):
            pl.semaphore_signal(barrier, inc=1, device_id=(gx, lax.rem(gy + d, inner)),
                                device_id_type=MESH)

        base = (gx * inner + gy) * face_dev
        index_tables(faces_ref[...], base, count, face_dev, nx, ny, idx_v)
        to_smem = pltpu.make_async_copy(idx_v, idx, idx_sem)
        to_smem.start()
        for g in range(face_dev // 8):
            for j in range(groups):
                tile_rows[(g * groups + j) * 8 : (g * groups + j + 1) * 8, :] = heat_ref[
                    g * 8 : g * 8 + 8, j * LANES : (j + 1) * LANES
                ]
        for f in range(face_dev):
            start = (f // 8) * groups * 8 + f % 8
            table[f] = tile_rows[pl.ds(start, groups, stride=8), :]
        to_smem.wait()
        for r in range(nx):
            send0[r] = table[idx[17, r]]
        for r in range(ny):
            send0[nx + r] = table[idx[18, r]]
        pl.semaphore_wait(barrier, outer + inner - 2)

        def remote(src, dst, ssem, rsem, device):
            return pltpu.make_async_remote_copy(
                src_ref=src, dst_ref=dst, send_sem=ssem, recv_sem=rsem,
                device_id=device, device_id_type=MESH,
            )

        first = [
            remote(send0.at[pl.ds(0, nx)], recv0.at[pl.ds(0, nx)], s0_sem.at[0], r0_sem.at[0], x_prev),
            remote(send0.at[pl.ds(nx, ny)], recv0.at[pl.ds(nx, ny)], s0_sem.at[1], r0_sem.at[1], y_prev),
        ]
        for c in first:
            c.start()

        def split(e, carry):
            raw_copy(e).wait()
            a = raw[e]
            h = a.astype(BF16)
            high[e] = h
            low[e] = (a - h.astype(F32)).astype(BF16)
            return carry

        lax.fori_loop(0, count, split, 0)
        for c in first:
            c.wait_recv()
        for r in range(nx + ny):
            table[face_dev + r] = recv0[r]

        def start_trace(e, carry):
            for k in range(6):
                v0[k * count + e] = table[idx[6 + k, e]]
            return carry

        lax.fori_loop(0, count, start_trace, 0, unroll=UNROLL)

        left = lax.broadcasted_iota(jnp.int32, (8, LANES), 1) < HALF

        def swap(a):
            return pltpu.roll(a, HALF, 1)

        def multiply(vec):
            def body(e, acc):
                evens, odds = [], []
                tiles = [vec[k * count + e] for k in range(6)]
                for axis in range(3):
                    a, b = tiles[2 * axis], tiles[2 * axis + 1]
                    evens.append(jnp.where(left, a, swap(b)))
                    odds.append(jnp.where(left, swap(a), b))
                x = jnp.concatenate(
                    [jnp.concatenate(evens, axis=1), jnp.concatenate(odds, axis=1)], axis=0
                )
                xh = x.astype(BF16)
                xl = (x - xh.astype(F32)).astype(BF16)
                both = jnp.concatenate([xh, xl], axis=0)
                p = jnp.dot(both, high[e], preferred_element_type=F32)
                q = jnp.dot(xh, low[e], preferred_element_type=F32)
                y = p[0:16] + (p[16:32] + q)
                for axis in range(3):
                    ev = y[0:8, axis * LANES : (axis + 1) * LANES]
                    od = y[8:16, axis * LANES : (axis + 1) * LANES]
                    fa = jnp.where(left, ev, swap(od))
                    fb = jnp.where(left, swap(ev), od)
                    flux[2 * axis * count + e] = fa
                    flux[(2 * axis + 1) * count + e] = fb
                    acc = acc + (fa * tiles[2 * axis] + fb * tiles[2 * axis + 1])
                return acc

            return lax.fori_loop(0, count, body, jnp.zeros((8, LANES), F32), unroll=UNROLL)

        spots = [0, nx, 2 * nx, 2 * nx + ny]
        plan = [(0, nx, x_prev, 1), (1, nx, x_next, 0), (2, ny, y_prev, 3), (3, ny, y_next, 2)]

        def exchange(phase, kinds):
            copies = []
            for kind, rows, target, lands in plan:
                if kind not in kinds:
                    continue
                for r in range(rows):
                    sends[phase, spots[kind] + r] = flux[idx[12 + kind, r]]
                copies.append(
                    remote(
                        sends.at[phase, pl.ds(spots[kind], rows)],
                        recvs.at[phase, pl.ds(spots[lands], rows)],
                        ss_sem.at[phase, kind], rr_sem.at[phase, lands], target,
                    )
                )
                copies[-1].start()
            return copies

        def landed(phase, copies, kinds):
            for c in copies:
                c.wait_recv()
            for kind, rows, _, _ in plan:
                if kind in kinds:
                    for r in range(rows):
                        flux[slots + spots[kind] + r] = recvs[phase, spots[kind] + r]

        def halves(tile):
            even = jnp.sum(jnp.where(left, tile, 0.0), axis=1, keepdims=True)
            odd = jnp.sum(jnp.where(left, 0.0, tile), axis=1, keepdims=True)
            return even, odd

        lane = lax.broadcasted_iota(jnp.int32, (8, LANES), 1)

        def packed(tiles):
            out = jnp.zeros((8, LANES), F32)
            for m, t in enumerate(tiles):
                even, odd = halves(t)
                out = jnp.where(lane == 2 * m, even, out)
                out = jnp.where(lane == 2 * m + 1, odd, out)
            return out

        def unpacked(total, m):
            return jnp.where(left, total[:, 2 * m : 2 * m + 1], total[:, 2 * m + 1 : 2 * m + 2])

        def sum_x_start(turn, value):
            txs[turn] = value
            copies = []
            for d in range(1, outer):
                copies.append(remote(txs.at[turn], rxx.at[turn, d - 1], xs_sem.at[turn, d - 1],
                                     xr_sem.at[turn, d - 1], (lax.rem(gx + d, outer), gy)))
                copies[-1].start()
            return copies

        def sum_x_end(turn, copies):
            for c in copies:
                c.wait_recv()
            out = txs[turn]
            for d in range(1, outer):
                out = out + rxx[turn, d - 1]
            return out

        def sum_y_start(turn, value):
            txy[turn] = value
            copies = []
            for d in range(1, inner):
                copies.append(remote(txy.at[turn], rxy.at[turn, d - 1], ys_sem.at[turn, d - 1],
                                     yr_sem.at[turn, d - 1], (gx, lax.rem(gy + d, inner))))
                copies[-1].start()
            return copies

        def sum_y_end(turn, copies):
            for c in copies:
                c.wait_recv()
            out = txy[turn]
            for d in range(1, inner):
                out = out + rxy[turn, d - 1]
            return out

        zero = jnp.zeros((8, LANES), F32)

        every = (0, 1, 2, 3)
        delta0 = multiply(v0)
        swap1 = exchange(0, every)
        gamma0 = zero
        for k in lows:
            for e in range(count):
                gamma0 = gamma0 + v0[k * count + e] * v0[k * count + e]
        ax1 = sum_x_start(0, packed([gamma0, delta0]))
        landed(0, swap1, every)

        def assemble(dst, e):
            for k in range(6):
                dst[k * count + e] = flux[k * count + e] + flux[idx[k, e]]

        def asm1(e, carry):
            assemble(v1, e)
            return carry

        lax.fori_loop(0, count, asm1, 0, unroll=UNROLL)
        ay1 = sum_y_start(0, sum_x_end(0, ax1))

        dot_g = multiply(v1)
        swap2 = exchange(1, every)
        total = sum_y_end(0, ay1)
        gamma0 = unpacked(total, 0)
        delta0 = unpacked(total, 1)
        alpha0 = gamma0 / delta0
        landed(1, swap2, every)

        def asm2(e, acc):
            acc = list(acc)
            for k in range(6):
                s = k * count + e
                val = flux[s] + flux[idx[k, e]]
                one = v1[s]
                w = one - alpha0 * val
                q1[s] = w
                v2[s] = val
                if k in lows:
                    r1 = v0[s] - alpha0 * one
                    terms = (r1 * r1, r1 * w, w * w, r1 * one, w * one, one * one, w * val)
                    acc = [a + t for a, t in zip(acc, terms)]
            return tuple(acc)

        dots = lax.fori_loop(0, count, asm2, (zero,) * 7, unroll=UNROLL)
        early = packed([*dots, dot_g])

        dot_e = multiply(q1)
        even, odd = halves(dot_e)
        early = jnp.where(lane == 16, even, early)
        early = jnp.where(lane == 17, odd, early)
        ax2 = sum_x_start(1, early)
        swap3 = exchange(2, (1, 3))
        ay2 = sum_y_start(1, sum_x_end(1, ax2))
        landed(2, swap3, (0, 2))

        def asm3(e, carry):
            for k in lows:
                s = k * count + e
                flux[s] = flux[s] + flux[idx[k, e]]
            return carry

        lax.fori_loop(0, count, asm3, 0, unroll=UNROLL)
        total = sum_y_end(1, ay2)
        g1, d1, ww, rv, wv, vv, f, g, ee = [unpacked(total, m) for m in range(9)]
        b0 = g1 / gamma0
        pap = d1 + 2.0 * b0 * rv + b0 * b0 * delta0
        a1 = g1 / pap
        rs = d1 + b0 * rv
        s2 = ww + b0 * (2.0 * wv + b0 * vv)
        g2 = g1 - 2.0 * a1 * rs + a1 * a1 * s2
        b1 = g2 / g1
        rar = d1 - 2.0 * a1 * (ww + b0 * wv) + a1 * a1 * (ee + b0 * (2.0 * f + b0 * g))
        pap2 = rar + 2.0 * b1 * (rs - a1 * s2) + b1 * b1 * pap
        a2 = g2 / pap2

        def finish(fc, carry):
            s = idx[16, fc]
            x0 = v0[s]
            one = v1[s]
            two = v2[s]
            r1 = x0 - alpha0 * one
            w = one - alpha0 * two
            p1 = r1 + b0 * x0
            s1 = w + b0 * one
            r2 = r1 - a1 * s1
            w2 = w - a1 * (flux[s] + b0 * two)
            p2 = r2 + b1 * p1
            sol_ref[fc] = alpha0 * x0 + a1 * p1 + a2 * p2
            res_ref[fc] = r2 - a2 * (w2 + b1 * s1)
            return carry

        lax.fori_loop(0, face_dev, finish, 0, unroll=2)
        for c in [*first, *swap1, *swap2, *swap3, *ax1, *ay1, *ax2, *ay2]:
            c.wait_send()

    return kernel


def local(heat_source, stiffness, element_faces):
    face_dev, width = heat_source.shape
    count, order = stiffness.shape[0], stiffness.shape[1]
    groups = width // LANES
    outer = lax.axis_size("gx")
    inner = lax.axis_size("gy")
    nx, ny = EY * EZ, EX * EZ
    slots = 6 * count
    ext = 2 * (nx + ny)
    tile = (groups, LANES)
    vmem = lambda *s: pltpu.VMEM(s, F32)
    dma = lambda *s: pltpu.SemaphoreType.DMA(s)
    out = jax.ShapeDtypeStruct((face_dev, *tile), F32)
    sol, res = pl.pallas_call(
        make_kernel(outer, inner, count, face_dev, groups, nx, ny),
        name="cg",
        out_shape=(out, out),
        in_specs=[
            pl.BlockSpec(memory_space=pltpu.VMEM),
            pl.BlockSpec(memory_space=pltpu.VMEM),
            pl.BlockSpec(memory_space=pl.ANY),
        ],
        out_specs=(pl.BlockSpec(memory_space=pltpu.VMEM),) * 2,
        scratch_shapes=[
            vmem(count, order, order),
            pltpu.VMEM((count, order, order), BF16),
            pltpu.VMEM((count, order, order), BF16),
            vmem(face_dev * groups, LANES),
            vmem(face_dev + nx + ny, *tile),
            vmem(slots, *tile),
            vmem(slots, *tile),
            vmem(slots, *tile),
            vmem(slots + ext, *tile),
            vmem(slots, *tile),
            pltpu.VMEM((24, LANES), jnp.int32),
            pltpu.SMEM((24, LANES), jnp.int32),
            vmem(nx + ny, *tile),
            vmem(nx + ny, *tile),
            vmem(3, ext, *tile),
            vmem(3, ext, *tile),
            vmem(2, *tile),
            vmem(2, outer - 1, *tile),
            vmem(2, inner - 1, *tile),
            vmem(2, *tile),
            dma(count), pltpu.SemaphoreType.DMA,
            dma(2), dma(2), dma(3, 4), dma(3, 4),
            dma(2, outer - 1), dma(2, outer - 1), dma(2, inner - 1), dma(2, inner - 1),
        ],
        compiler_params=pltpu.CompilerParams(
            collective_id=0, has_side_effects=True, vmem_limit_bytes=48 * 1024 * 1024
        ),
    )(heat_source, element_faces, stiffness)
    return sol.reshape(face_dev, width), res.reshape(face_dev, width)


def solution(mesh):
    return jax.shard_map(
        local,
        mesh=mesh,
        in_specs=(P(("gx", "gy"), None), P(("gx", "gy"), None, None), P(("gx", "gy"), None)),
        out_specs=(P(("gx", "gy"), None), P(("gx", "gy"), None)),
        check_vma=False,
    )
```

time: 283 us -> 40.1 us (0.14)
  blocking collectives: 117 us -> 0 us
  matrix products: 86.4 us -> 0 us
  Pallas kernels: 0 us -> 36.8 us
  local copies, waits for them, and re-layouts: 34.2 us -> 2.5 us
  starting transfers between devices: 16.1 us -> 0 us
  waiting for transfers between devices: 14.2 us -> 0 us
  other arithmetic: 12.6 us -> 0 us
    psum x3 -> x0, blocking collectives: 117 us -> none  [pair_sums(): lax.psum((source_sum(residual, residual), source_sum(residual, applied)),...]
    dot_general x3 -> x0, matrix products: 86.4 us -> none  [operate(): jnp.einsum('ekbjc,ejsc->eksb', matrix, blocks, precision=lax.Precision.HI...]
    pallas_call x0 -> x1, Pallas kernels: none -> 36.8 us  [local(): pl.pallas_call(make_kernel(outer, inner, count, face_dev, groups, nx, ny)...]
    reshape x7 -> x1, local copies, waits for them, and re-layouts: 18.5 us -> 0.81 us  [local(): return (sol.reshape(face_dev, width), res.reshape(face_dev, width))]
    ppermute x14 -> x0, starting transfers between devices: 16.1 us -> none  [passed_along(): return lax.ppermute(value, axis, pairs)]
    ppermute x14 -> x0, waiting for transfers between devices: 14.2 us -> none  [passed_along(): return lax.ppermute(value, axis, pairs)]
    gather x17 -> x0, local copies, waits for them, and re-layouts: 12.2 us -> none  [the longest x6 5.28 us: operate(): incoming_x, incoming_y = send_traces(vector[wanted_x], vector[wanted_y])]
    scatter-add x9 -> x0, other arithmetic: 8.77 us -> none  [the longest x6 4.54 us: operate(): return result.at[wanted_x].add(back_x).at[wanted_y].add(back_y)]
  transfers between devices with their start and end apart: 14 -> 0, of which waited for: 8 -> 0; matrix products, arithmetic and copies ran while one was open for 10% -> 0% of each run, Pallas kernels for 0% -> 0%
where the time goes in v1:
time: 40.1 us; the launch traced here: 39.9 us
  Pallas kernels  36.8 us (92%)
  local copies, waits for them, and re-layouts  2.5 us (6%)
  between operations  0.64 us (2%)
    pallas_call x1, Pallas kernels, local(): pl.pallas_call(make_kernel(outer, inner, count, face_dev, groups, nx, ny)...  36.8 us
    unnamed x3, local copies, waits for them, and re-layouts  1.69 us
    reshape x1, local copies, waits for them, and re-layouts, local(): return (sol.reshape(face_dev, width), res.reshape(face_dev, width))  0.81 us

profile of v1, /device:TPU:0, one launch (start us, length us, event | category | flops | bytes accessed | tf_op | source)
XLA Modules:
  0.0 39.9 jit_solution(10706310163958072358)
XLA Ops:
  0.6 0.8 %copy.5.faces_ref = s32[16,6]{1,0:T(8,128)S(1)} copy(s32[16,6]{0,1:T(8,128)} %param.5) | data formatting | bytes 768 | tf_op args[2]
  1.4 0.0 copy-start
  1.4 0.9 %copy-done = f32[48,1024]{1,0:T(8,128)S(1)} copy-done((f32[48,1024]{1,0:T(8,128)S(1)}, f32[48,1024]{1,0:T(8,128)}, u32[]{:S(2)}) %copy-start) | copy-done | bytes 196632
  2.3 36.8 %cg.1 = (f32[48,8,128]{2,1,0:T(8,128)S(1)}, f32[48,8,128]{2,1,0:T(8,128)S(1)}) custom-call(f32[48,1024]{1,0:T(8,128)S(1)} %copy-done, s32[16,6]{1,0:T(8,128)S(1)} %copy.5.faces_ref, f32[16,384,384]{2,1,0:T(8,128)} %stiff_ref.1), custom_call_target="tpu_custom_call" | custom-call | tf_op jit(solution)/shard_map/cg/pallas_call | solution.py:383
  39.1 0.8 %copy_bitcast_fusion = (f32[48,1024]{1,0:T(8,128)}, f32[48,1024]{1,0:T(8,128)}) fusion(f32[6,8,8,128]{3,2,1,0:T(8,128)S(1)} %bitcast.7, f32[6,8,8,128]{3,2,1,0:T(8,128)S(1)} %bitcast.6), kind=kLoop, calls=%fused_computation | loop fusion | bytes 786432 | tf_op jit(solution)/shard_map/reshape | solution.py:422
Async XLA Ops:
  1.4 0.9 %copy-start = (f32[48,1024]{1,0:T(8,128)S(1)}, f32[48,1024]{1,0:T(8,128)}, u32[]{:S(2)}) copy-start(f32[48,1024]{1,0:T(8,128)} %heat_ref.1) | copy-start | bytes 589828

commit v2 on v1

--- a/solution.py
+++ b/solution.py
@@ -73,12 +73,13 @@
 def make_kernel(outer, inner, count, face_dev, groups, nx, ny):
     slots = 6 * count
     lows = (0, 2, 4)
-
-    def kernel(heat_ref, faces_ref, stiff_ref, sol_ref, res_ref,
-               raw, high, low, tile_rows, table, v0, v1, v2, flux, q1,
-               idx_v, idx, send0, recv0, sends, recvs, txs, rxx, rxy, txy,
-               raw_sem, idx_sem, s0_sem, r0_sem, ss_sem, rr_sem,
-               xs_sem, xr_sem, ys_sem, yr_sem):
+    parts = outer * inner
+
+    def kernel(heat_hbm, faces_hbm, stiff_ref, sol_ref, res_ref,
+               heat_ref, faces_ref, raw, high, low, diag, tile_rows, table, v0, v1, v2, flux, q1,
+               idx_v, idx, send0, recv0, sends, recvs, sum_tx, sum_rx,
+               in_sem, raw_sem, idx_sem, s0_sem, r0_sem, ss_sem, rr_sem,
+               sum_ss, sum_rs):
         gx = lax.axis_index("gx")
         gy = lax.axis_index("gy")
         x_next = (lax.rem(gx + 1, outer), gy)
@@ -86,23 +87,29 @@
         y_next = (gx, lax.rem(gy + 1, inner))
         y_prev = (gx, lax.rem(gy + inner - 1, inner))
 
+        get_heat = pltpu.make_async_copy(heat_hbm, heat_ref, in_sem.at[0])
+        get_faces = pltpu.make_async_copy(faces_hbm, faces_ref, in_sem.at[1])
+        get_faces.start()
+        get_heat.start()
+
+        def other(d):
+            return (lax.rem(gx + d // inner, outer), lax.rem(gy + d % inner, inner))
+
         def raw_copy(e):
             return pltpu.make_async_copy(stiff_ref.at[e], raw.at[e], raw_sem.at[e])
 
         for e in range(count):
             raw_copy(e).start()
         barrier = pltpu.get_barrier_semaphore()
-        for d in range(1, outer):
-            pl.semaphore_signal(barrier, inc=1, device_id=(lax.rem(gx + d, outer), gy),
-                                device_id_type=MESH)
-        for d in range(1, inner):
-            pl.semaphore_signal(barrier, inc=1, device_id=(gx, lax.rem(gy + d, inner)),
-                                device_id_type=MESH)
+        for d in range(1, parts):
+            pl.semaphore_signal(barrier, inc=1, device_id=other(d), device_id_type=MESH)
 
         base = (gx * inner + gy) * face_dev
+        get_faces.wait()
         index_tables(faces_ref[...], base, count, face_dev, nx, ny, idx_v)
         to_smem = pltpu.make_async_copy(idx_v, idx, idx_sem)
         to_smem.start()
+        get_heat.wait()
         for g in range(face_dev // 8):
             for j in range(groups):
                 tile_rows[(g * groups + j) * 8 : (g * groups + j + 1) * 8, :] = heat_ref[
@@ -116,7 +123,7 @@
             send0[r] = table[idx[17, r]]
         for r in range(ny):
             send0[nx + r] = table[idx[18, r]]
-        pl.semaphore_wait(barrier, outer + inner - 2)
+        pl.semaphore_wait(barrier, parts - 1)
 
         def remote(src, dst, ssem, rsem, device):
             return pltpu.make_async_remote_copy(
@@ -131,12 +138,25 @@
         for c in first:
             c.start()
 
+        eye = lax.broadcasted_iota(jnp.int32, (LANES, LANES), 0) == lax.broadcasted_iota(
+            jnp.int32, (LANES, LANES), 1
+        )
+
         def split(e, carry):
             raw_copy(e).wait()
-            a = raw[e]
-            h = a.astype(BF16)
-            high[e] = h
-            low[e] = (a - h.astype(F32)).astype(BF16)
+            for r in range(3):
+                rows = pl.ds(r * LANES, LANES)
+                for c in range(3):
+                    columns = pl.ds(c * LANES, LANES)
+                    a = raw[e, rows, columns]
+                    if r == c:
+                        diag[e, :, columns] = jnp.sum(
+                            jnp.where(eye, a, 0.0), axis=0, keepdims=True
+                        )
+                        a = jnp.where(eye, 0.0, a)
+                    h = a.astype(BF16)
+                    high[e, rows, columns] = h
+                    low[e, rows, columns] = (a - h.astype(F32)).astype(BF16)
             return carry
 
         lax.fori_loop(0, count, split, 0)
@@ -173,7 +193,7 @@
                 both = jnp.concatenate([xh, xl], axis=0)
                 p = jnp.dot(both, high[e], preferred_element_type=F32)
                 q = jnp.dot(xh, low[e], preferred_element_type=F32)
-                y = p[0:16] + (p[16:32] + q)
+                y = x * diag[e] + (p[0:16] + (p[16:32] + q))
                 for axis in range(3):
                     ev = y[0:8, axis * LANES : (axis + 1) * LANES]
                     od = y[8:16, axis * LANES : (axis + 1) * LANES]
@@ -221,50 +241,37 @@
 
         lane = lax.broadcasted_iota(jnp.int32, (8, LANES), 1)
 
-        def packed(tiles):
-            out = jnp.zeros((8, LANES), F32)
-            for m, t in enumerate(tiles):
+        sub = lax.broadcasted_iota(jnp.int32, (8, LANES), 0)
+        spot = lane % 16
+        mine = lane // 16 == sub
+
+        def packed(tiles, out=None, first=0):
+            out = jnp.zeros((8, LANES), F32) if out is None else out
+            for m, t in enumerate(tiles, first):
                 even, odd = halves(t)
-                out = jnp.where(lane == 2 * m, even, out)
-                out = jnp.where(lane == 2 * m + 1, odd, out)
+                out = jnp.where(spot == 2 * m, even, out)
+                out = jnp.where(spot == 2 * m + 1, odd, out)
             return out
 
-        def unpacked(total, m):
-            return jnp.where(left, total[:, 2 * m : 2 * m + 1], total[:, 2 * m + 1 : 2 * m + 2])
-
-        def sum_x_start(turn, value):
-            txs[turn] = value
+        def unpacked(row, m):
+            own = jnp.where(mine, jnp.broadcast_to(row, (8, LANES)), 0.0)
+            even = jnp.sum(jnp.where(spot == 2 * m, own, 0.0), axis=1, keepdims=True)
+            odd = jnp.sum(jnp.where(spot == 2 * m + 1, own, 0.0), axis=1, keepdims=True)
+            return jnp.where(left, even, odd)
+
+        def sum_start(turn, value):
+            sum_tx[turn] = jnp.sum(jnp.where(mine, value, 0.0), axis=0, keepdims=True)
             copies = []
-            for d in range(1, outer):
-                copies.append(remote(txs.at[turn], rxx.at[turn, d - 1], xs_sem.at[turn, d - 1],
-                                     xr_sem.at[turn, d - 1], (lax.rem(gx + d, outer), gy)))
+            for d in range(1, parts):
+                copies.append(remote(sum_tx.at[turn], sum_rx.at[turn, d - 1], sum_ss.at[turn, d - 1],
+                                     sum_rs.at[turn, d - 1], other(d)))
                 copies[-1].start()
             return copies
 
-        def sum_x_end(turn, copies):
+        def sum_end(turn, copies):
             for c in copies:
                 c.wait_recv()
-            out = txs[turn]
-            for d in range(1, outer):
-                out = out + rxx[turn, d - 1]
-            return out
-
-        def sum_y_start(turn, value):
-            txy[turn] = value
-            copies = []
-            for d in range(1, inner):
-                copies.append(remote(txy.at[turn], rxy.at[turn, d - 1], ys_sem.at[turn, d - 1],
-                                     yr_sem.at[turn, d - 1], (gx, lax.rem(gy + d, inner))))
-                copies[-1].start()
-            return copies
-
-        def sum_y_end(turn, copies):
-            for c in copies:
-                c.wait_recv()
-            out = txy[turn]
-            for d in range(1, inner):
-                out = out + rxy[turn, d - 1]
-            return out
+            return sum_tx[turn] + jnp.sum(sum_rx[turn], axis=0)
 
         zero = jnp.zeros((8, LANES), F32)
 
@@ -275,7 +282,7 @@
         for k in lows:
             for e in range(count):
                 gamma0 = gamma0 + v0[k * count + e] * v0[k * count + e]
-        ax1 = sum_x_start(0, packed([gamma0, delta0]))
+        sum1 = sum_start(0, packed([gamma0, delta0]))
         landed(0, swap1, every)
 
         def assemble(dst, e):
@@ -287,11 +294,10 @@
             return carry
 
         lax.fori_loop(0, count, asm1, 0, unroll=UNROLL)
-        ay1 = sum_y_start(0, sum_x_end(0, ax1))
 
         dot_g = multiply(v1)
         swap2 = exchange(1, every)
-        total = sum_y_end(0, ay1)
+        total = sum_end(0, sum1)
         gamma0 = unpacked(total, 0)
         delta0 = unpacked(total, 1)
         alpha0 = gamma0 / delta0
@@ -308,20 +314,16 @@
                 v2[s] = val
                 if k in lows:
                     r1 = v0[s] - alpha0 * one
-                    terms = (r1 * r1, r1 * w, w * w, r1 * one, w * one, one * one, w * val)
+                    terms = (r1 * r1, r1 * w, w * w, w * one, one * one, w * val)
                     acc = [a + t for a, t in zip(acc, terms)]
             return tuple(acc)
 
-        dots = lax.fori_loop(0, count, asm2, (zero,) * 7, unroll=UNROLL)
+        dots = lax.fori_loop(0, count, asm2, (zero,) * 6, unroll=UNROLL)
         early = packed([*dots, dot_g])
 
         dot_e = multiply(q1)
-        even, odd = halves(dot_e)
-        early = jnp.where(lane == 16, even, early)
-        early = jnp.where(lane == 17, odd, early)
-        ax2 = sum_x_start(1, early)
+        sum2 = sum_start(1, packed([dot_e], early, 7))
         swap3 = exchange(2, (1, 3))
-        ay2 = sum_y_start(1, sum_x_end(1, ax2))
         landed(2, swap3, (0, 2))
 
         def asm3(e, carry):
@@ -331,8 +333,9 @@
             return carry
 
         lax.fori_loop(0, count, asm3, 0, unroll=UNROLL)
-        total = sum_y_end(1, ay2)
-        g1, d1, ww, rv, wv, vv, f, g, ee = [unpacked(total, m) for m in range(9)]
+        total = sum_end(1, sum2)
+        g1, d1, ww, wv, vv, f, g, ee = [unpacked(total, m) for m in range(8)]
+        rv = -g1 / alpha0
         b0 = g1 / gamma0
         pap = d1 + 2.0 * b0 * rv + b0 * b0 * delta0
         a1 = g1 / pap
@@ -361,7 +364,7 @@
             return carry
 
         lax.fori_loop(0, face_dev, finish, 0, unroll=2)
-        for c in [*first, *swap1, *swap2, *swap3, *ax1, *ay1, *ax2, *ay2]:
+        for c in [*first, *swap1, *swap2, *swap3, *sum1, *sum2]:
             c.wait_send()
 
     return kernel
@@ -385,15 +388,18 @@
         name="cg",
         out_shape=(out, out),
         in_specs=[
-            pl.BlockSpec(memory_space=pltpu.VMEM),
-            pl.BlockSpec(memory_space=pltpu.VMEM),
-            pl.BlockSpec(memory_space=pl.ANY),
+            pl.BlockSpec(memory_space=pltpu.HBM),
+            pl.BlockSpec(memory_space=pltpu.HBM),
+            pl.BlockSpec(memory_space=pltpu.HBM),
         ],
         out_specs=(pl.BlockSpec(memory_space=pltpu.VMEM),) * 2,
         scratch_shapes=[
+            vmem(face_dev, width),
+            pltpu.VMEM(element_faces.shape, jnp.int32),
             vmem(count, order, order),
             pltpu.VMEM((count, order, order), BF16),
             pltpu.VMEM((count, order, order), BF16),
+            vmem(count, 1, order),
             vmem(face_dev * groups, LANES),
             vmem(face_dev + nx + ny, *tile),
             vmem(slots, *tile),
@@ -407,16 +413,15 @@
             vmem(nx + ny, *tile),
             vmem(3, ext, *tile),
             vmem(3, ext, *tile),
-            vmem(2, *tile),
-            vmem(2, outer - 1, *tile),
-            vmem(2, inner - 1, *tile),
-            vmem(2, *tile),
+            vmem(2, 1, LANES),
+            vmem(2, outer * inner - 1, 1, LANES),
+            dma(2),
             dma(count), pltpu.SemaphoreType.DMA,
             dma(2), dma(2), dma(3, 4), dma(3, 4),
-            dma(2, outer - 1), dma(2, outer - 1), dma(2, inner - 1), dma(2, inner - 1),
+            dma(2, outer * inner - 1), dma(2, outer * inner - 1),
         ],
         compiler_params=pltpu.CompilerParams(
-            collective_id=0, has_side_effects=True, vmem_limit_bytes=48 * 1024 * 1024
+            collective_id=0, has_side_effects=True, vmem_limit_bytes=67043328
         ),
     )(heat_source, element_faces, stiffness)
     return sol.reshape(face_dev, width), res.reshape(face_dev, width)

time: 40.1 us -> 41.1 us (1.025)
  local copies, waits for them, and re-layouts: 2.5 us -> 3.2 us
    reshape x1, local copies, waits for them, and re-layouts: 0.81 us -> 1.84 us  [local(): return (sol.reshape(face_dev, width), res.reshape(face_dev, width))]
    unnamed x3 -> x1, local copies, waits for them, and re-layouts: 1.69 us -> 1.36 us
where the time goes in v2:
time: 41.1 us; the launch traced here: 40.9 us
  Pallas kernels  37.1 us (90%)
  local copies, waits for them, and re-layouts  3.2 us (8%)
  between operations  0.64 us (2%)
    pallas_call x1, Pallas kernels, local(): pl.pallas_call(make_kernel(outer, inner, count, face_dev, groups, nx, ny)...  37.1 us
    reshape x1, local copies, waits for them, and re-layouts, local(): return (sol.reshape(face_dev, width), res.reshape(face_dev, width))  1.84 us
    unnamed x1, local copies, waits for them, and re-layouts  1.36 us

profile of v2, /device:TPU:0, one launch (start us, length us, event | category | flops | bytes accessed | tf_op | source)
XLA Modules:
  0.0 40.9 jit_solution(11062503143476316638)
XLA Ops:
  0.6 1.4 %copy.5.faces_hbm = s32[16,6]{1,0:T(8,128)} copy(s32[16,6]{0,1:T(8,128)} %param.5) | data formatting | bytes 768 | tf_op args[2]
  2.0 37.1 %cg.1 = (f32[48,8,128]{2,1,0:T(8,128)}, f32[48,8,128]{2,1,0:T(8,128)}) custom-call(f32[48,1024]{1,0:T(8,128)} %heat_hbm.1, s32[16,6]{1,0:T(8,128)} %copy.5.faces_hbm, f32[16,384,384]{2,1,0:T(8,128)} %stiff_ref.1), custom_call_target="tpu_custom_call" | custom-call | tf_op jit(solution)/shard_map/cg/pallas_call | solution.py:386
  39.1 1.8 %copy_bitcast_fusion = (f32[48,1024]{1,0:T(8,128)}, f32[48,1024]{1,0:T(8,128)}) fusion(f32[6,8,8,128]{3,2,1,0:T(8,128)} %bitcast.7, f32[6,8,8,128]{3,2,1,0:T(8,128)} %bitcast.6), kind=kLoop, calls=%fused_computation | loop fusion | bytes 786432 | tf_op jit(solution)/shard_map/reshape | solution.py:427

commit v3 on v2

--- a/solution.py
+++ b/solution.py
@@ -22,8 +22,8 @@
     lane = lax.broadcasted_iota(jnp.int32, (count, count), 1)
     eye = sub == lane
     slots = 6 * count
-    cols = [faces[:, k : k + 1] for k in range(6)]
-    rows = [jnp.sum(jnp.where(eye, c, 0), axis=0, keepdims=True) for c in cols]
+    rows = [faces[k : k + 1, :] for k in range(6)]
+    cols = [jnp.sum(jnp.where(eye, r, 0), axis=1, keepdims=True) for r in rows]
     idx[...] = jnp.zeros(idx.shape, jnp.int32)
     sizes = [nx, nx, ny, ny]
     starts = [slots, slots + nx, slots + 2 * nx, slots + 2 * nx + ny]
@@ -204,7 +204,7 @@
                     acc = acc + (fa * tiles[2 * axis] + fb * tiles[2 * axis + 1])
                 return acc
 
-            return lax.fori_loop(0, count, body, jnp.zeros((8, LANES), F32), unroll=UNROLL)
+            return lax.fori_loop(0, count, body, jnp.zeros((8, LANES), F32), unroll=True)
 
         spots = [0, nx, 2 * nx, 2 * nx + ny]
         plan = [(0, nx, x_prev, 1), (1, nx, x_next, 0), (2, ny, y_prev, 3), (3, ny, y_next, 2)]
@@ -395,7 +395,7 @@
         out_specs=(pl.BlockSpec(memory_space=pltpu.VMEM),) * 2,
         scratch_shapes=[
             vmem(face_dev, width),
-            pltpu.VMEM(element_faces.shape, jnp.int32),
+            pltpu.VMEM((6, count), jnp.int32),
             vmem(count, order, order),
             pltpu.VMEM((count, order, order), BF16),
             pltpu.VMEM((count, order, order), BF16),
@@ -423,7 +423,7 @@
         compiler_params=pltpu.CompilerParams(
             collective_id=0, has_side_effects=True, vmem_limit_bytes=67043328
         ),
-    )(heat_source, element_faces, stiffness)
+    )(heat_source, element_faces.T, stiffness)
     return sol.reshape(face_dev, width), res.reshape(face_dev, width)
 
 

time: 41.1 us -> 34.3 us (0.83)
  Pallas kernels: 37.1 us -> 31.6 us
  local copies, waits for them, and re-layouts: 3.2 us -> 1.84 us
    pallas_call x1, Pallas kernels: 37.1 us -> 31.6 us  [local(): pl.pallas_call(make_kernel(outer, inner, count, face_dev, groups, nx, ny)...]
    unnamed x1 -> x0, local copies, waits for them, and re-layouts: 1.36 us -> none
where the time goes in v3:
time: 34.3 us; the launch traced here: 34.1 us
  Pallas kernels  31.6 us (92%)
  local copies, waits for them, and re-layouts  1.84 us (5%)
  between operations  0.64 us (2%)
    pallas_call x1, Pallas kernels, local(): pl.pallas_call(make_kernel(outer, inner, count, face_dev, groups, nx, ny)...  31.6 us
    reshape x1, local copies, waits for them, and re-layouts, local(): return (sol.reshape(face_dev, width), res.reshape(face_dev, width))  1.84 us

profile of v3, /device:TPU:0, one launch (start us, length us, event | category | flops | bytes accessed | tf_op | source)
XLA Modules:
  0.0 34.1 jit_solution(2610155218429902663)
XLA Ops:
  0.6 31.6 %cg.1 = (f32[48,8,128]{2,1,0:T(8,128)}, f32[48,8,128]{2,1,0:T(8,128)}) custom-call(f32[48,1024]{1,0:T(8,128)} %heat_hbm.1, s32[6,16]{1,0:T(8,128)} %bitcast.9, f32[16,384,384]{2,1,0:T(8,128)} %stiff_ref.1), custom_call_target="tpu_custom_call" | custom-call | tf_op jit(solution)/shard_map/cg/pallas_call | solution.py:386
  32.3 1.8 %copy_bitcast_fusion = (f32[48,1024]{1,0:T(8,128)}, f32[48,1024]{1,0:T(8,128)}) fusion(f32[6,8,8,128]{3,2,1,0:T(8,128)} %bitcast.8, f32[6,8,8,128]{3,2,1,0:T(8,128)} %bitcast.7), kind=kLoop, calls=%fused_computation | loop fusion | bytes 786432 | tf_op jit(solution)/shard_map/reshape | solution.py:427

commit v4 on v3

--- a/solution.py
+++ b/solution.py
@@ -76,7 +76,7 @@
     parts = outer * inner
 
     def kernel(heat_hbm, faces_hbm, stiff_ref, sol_ref, res_ref,
-               heat_ref, faces_ref, raw, high, low, diag, tile_rows, table, v0, v1, v2, flux, q1,
+               heat_ref, faces_ref, raw, high, low, diag, tile_rows, table, v0, v1, v2, flux, flux2, q1,
                idx_v, idx, send0, recv0, sends, recvs, sum_tx, sum_rx,
                in_sem, raw_sem, idx_sem, s0_sem, r0_sem, ss_sem, rr_sem,
                sum_ss, sum_rs):
@@ -160,56 +160,63 @@
             return carry
 
         lax.fori_loop(0, count, split, 0)
-        for c in first:
-            c.wait_recv()
-        for r in range(nx + ny):
-            table[face_dev + r] = recv0[r]
-
-        def start_trace(e, carry):
-            for k in range(6):
-                v0[k * count + e] = table[idx[6 + k, e]]
-            return carry
-
-        lax.fori_loop(0, count, start_trace, 0, unroll=UNROLL)
-
         left = lax.broadcasted_iota(jnp.int32, (8, LANES), 1) < HALF
 
         def swap(a):
             return pltpu.roll(a, HALF, 1)
 
-        def multiply(vec):
+        def product(tiles, e):
+            evens, odds = [], []
+            for a, b in zip(tiles[0::2], tiles[1::2]):
+                evens.append(jnp.where(left, a, swap(b)))
+                odds.append(jnp.where(left, swap(a), b))
+            x = jnp.concatenate(
+                [jnp.concatenate(evens, axis=1), jnp.concatenate(odds, axis=1)], axis=0
+            )
+            depth = x.shape[1]
+            xh = x.astype(BF16)
+            xl = (x - xh.astype(F32)).astype(BF16)
+            both = jnp.concatenate([xh, xl], axis=0)
+            p = jnp.dot(both, high[e, 0:depth, :], preferred_element_type=F32)
+            q = jnp.dot(xh, low[e, 0:depth, :], preferred_element_type=F32)
+            y = p[0:16] + (p[16:32] + q)
+            own = x * diag[e, :, 0:depth]
+            out = []
+            for axis in range(3):
+                at = slice(axis * LANES, (axis + 1) * LANES)
+                part = y[:, at] + own[:, at] if axis * LANES < depth else y[:, at]
+                ev, od = part[0:8], part[8:16]
+                out.append(jnp.where(left, ev, swap(od)))
+                out.append(jnp.where(left, swap(ev), od))
+            return out
+
+        def inside(new, tiles_of, init):
             def body(e, acc):
-                evens, odds = [], []
-                tiles = [vec[k * count + e] for k in range(6)]
-                for axis in range(3):
-                    a, b = tiles[2 * axis], tiles[2 * axis + 1]
-                    evens.append(jnp.where(left, a, swap(b)))
-                    odds.append(jnp.where(left, swap(a), b))
-                x = jnp.concatenate(
-                    [jnp.concatenate(evens, axis=1), jnp.concatenate(odds, axis=1)], axis=0
-                )
-                xh = x.astype(BF16)
-                xl = (x - xh.astype(F32)).astype(BF16)
-                both = jnp.concatenate([xh, xl], axis=0)
-                p = jnp.dot(both, high[e], preferred_element_type=F32)
-                q = jnp.dot(xh, low[e], preferred_element_type=F32)
-                y = x * diag[e] + (p[0:16] + (p[16:32] + q))
-                for axis in range(3):
-                    ev = y[0:8, axis * LANES : (axis + 1) * LANES]
-                    od = y[8:16, axis * LANES : (axis + 1) * LANES]
-                    fa = jnp.where(left, ev, swap(od))
-                    fb = jnp.where(left, swap(ev), od)
-                    flux[2 * axis * count + e] = fa
-                    flux[(2 * axis + 1) * count + e] = fb
-                    acc = acc + (fa * tiles[2 * axis] + fb * tiles[2 * axis + 1])
+                tiles, acc = tiles_of(e, acc)
+                for k, f in enumerate(product(tiles, e)):
+                    new[k * count + e] = f
                 return acc
 
-            return lax.fori_loop(0, count, body, jnp.zeros((8, LANES), F32), unroll=True)
+            return lax.fori_loop(0, count, body, init, unroll=True)
+
+        def edges(new, tiles_of, init):
+            def body(e, carry):
+                dot, acc = carry
+                tiles, full, acc = tiles_of(e, acc)
+                for k, f in enumerate(product(tiles, e)):
+                    s = k * count + e
+                    f = new[s] + f
+                    new[s] = f
+                    dot = dot + f * full[k]
+                return dot, acc
+
+            start = (jnp.zeros((8, LANES), F32), init)
+            return lax.fori_loop(0, count, body, start, unroll=True)
 
         spots = [0, nx, 2 * nx, 2 * nx + ny]
         plan = [(0, nx, x_prev, 1), (1, nx, x_next, 0), (2, ny, y_prev, 3), (3, ny, y_next, 2)]
 
-        def exchange(phase, kinds):
+        def exchange(phase, flux, kinds):
             copies = []
             for kind, rows, target, lands in plan:
                 if kind not in kinds:
@@ -226,7 +233,7 @@
                 copies[-1].start()
             return copies
 
-        def landed(phase, copies, kinds):
+        def landed(phase, flux, copies, kinds):
             for c in copies:
                 c.wait_recv()
             for kind, rows, _, _ in plan:
@@ -276,55 +283,116 @@
         zero = jnp.zeros((8, LANES), F32)
 
         every = (0, 1, 2, 3)
-        delta0 = multiply(v0)
-        swap1 = exchange(0, every)
-        gamma0 = zero
-        for k in lows:
-            for e in range(count):
-                gamma0 = gamma0 + v0[k * count + e] * v0[k * count + e]
+
+        def traces_in(e, acc):
+            tiles = []
+            for k in range(6):
+                at = idx[6 + k, e]
+                t = table[at]
+                if k in (1, 3):
+                    t = jnp.where(at < face_dev, t, 0.0)
+                if k in lows:
+                    acc = acc + t * t
+                v0[k * count + e] = t
+                tiles.append(t)
+            return tiles, acc
+
+        def traces_edge(e, acc):
+            tiles, full = [], [v0[k * count + e] for k in range(6)]
+            for k in range(4):
+                t = zero
+                if k in (1, 3):
+                    at = idx[6 + k, e]
+                    t = jnp.where(at < face_dev, 0.0, table[at])
+                    full[k] = full[k] + t
+                    v0[k * count + e] = full[k]
+                tiles.append(t)
+            return tiles, full, acc
+
+        gamma0 = inside(flux, traces_in, zero)
+        for c in first:
+            c.wait_recv()
+        for r in range(nx + ny):
+            table[face_dev + r] = recv0[r]
+        delta0, _ = edges(flux, traces_edge, 0)
+        swap1 = exchange(0, flux, every)
         sum1 = sum_start(0, packed([gamma0, delta0]))
-        landed(0, swap1, every)
-
-        def assemble(dst, e):
+
+        def one_in(e, acc):
+            tiles = []
             for k in range(6):
-                dst[k * count + e] = flux[k * count + e] + flux[idx[k, e]]
-
-        def asm1(e, carry):
-            assemble(v1, e)
-            return carry
-
-        lax.fori_loop(0, count, asm1, 0, unroll=UNROLL)
-
-        dot_g = multiply(v1)
-        swap2 = exchange(1, every)
+                s = k * count + e
+                at = idx[k, e]
+                t = flux[s] + flux[at]
+                if k < 4:
+                    t = jnp.where(at < slots, t, 0.0)
+                v1[s] = t
+                tiles.append(t)
+            return tiles, acc
+
+        def one_edge(e, acc):
+            tiles, full = [], [v1[k * count + e] for k in range(6)]
+            for k in range(4):
+                s = k * count + e
+                at = idx[k, e]
+                t = jnp.where(at < slots, 0.0, flux[s] + flux[at])
+                full[k] = full[k] + t
+                v1[s] = full[k]
+                tiles.append(t)
+            return tiles, full, acc
+
+        inside(flux2, one_in, 0)
+        landed(0, flux, swap1, every)
+        dot_g, _ = edges(flux2, one_edge, 0)
+        swap2 = exchange(1, flux2, every)
         total = sum_end(0, sum1)
         gamma0 = unpacked(total, 0)
         delta0 = unpacked(total, 1)
         alpha0 = gamma0 / delta0
-        landed(1, swap2, every)
-
-        def asm2(e, acc):
-            acc = list(acc)
+
+        def dots_of(s, val, w, acc):
+            one = v1[s]
+            r1 = v0[s] - alpha0 * one
+            terms = (r1 * r1, r1 * w, w * w, w * one, one * one, w * val)
+            return tuple(a + t for a, t in zip(acc, terms))
+
+        def two_in(e, acc):
+            tiles = []
             for k in range(6):
                 s = k * count + e
-                val = flux[s] + flux[idx[k, e]]
-                one = v1[s]
-                w = one - alpha0 * val
+                at = idx[k, e]
+                val = flux2[s] + flux2[at]
+                w = v1[s] - alpha0 * val
+                if k < 4:
+                    w = jnp.where(at < slots, w, 0.0)
+                if k == 4:
+                    acc = dots_of(s, val, w, acc)
+                v2[s] = val
                 q1[s] = w
-                v2[s] = val
+                tiles.append(w)
+            return tiles, acc
+
+        def two_edge(e, acc):
+            tiles, full = [], [q1[k * count + e] for k in range(6)]
+            for k in range(4):
+                s = k * count + e
+                at = idx[k, e]
+                val = flux2[s] + flux2[at]
+                w = v1[s] - alpha0 * val
+                tiles.append(jnp.where(at < slots, 0.0, w))
+                full[k] = w
                 if k in lows:
-                    r1 = v0[s] - alpha0 * one
-                    terms = (r1 * r1, r1 * w, w * w, w * one, one * one, w * val)
-                    acc = [a + t for a, t in zip(acc, terms)]
-            return tuple(acc)
-
-        dots = lax.fori_loop(0, count, asm2, (zero,) * 6, unroll=UNROLL)
+                    v2[s] = val
+                    acc = dots_of(s, val, w, acc)
+            return tiles, full, acc
+
+        dots = inside(flux, two_in, (zero,) * 6)
+        landed(1, flux2, swap2, every)
+        dot_e, dots = edges(flux, two_edge, dots)
         early = packed([*dots, dot_g])
-
-        dot_e = multiply(q1)
         sum2 = sum_start(1, packed([dot_e], early, 7))
-        swap3 = exchange(2, (1, 3))
-        landed(2, swap3, (0, 2))
+        swap3 = exchange(2, flux, (1, 3))
+        landed(2, flux, swap3, (0, 2))
 
         def asm3(e, carry):
             for k in lows:
@@ -406,6 +474,7 @@
             vmem(slots, *tile),
             vmem(slots, *tile),
             vmem(slots + ext, *tile),
+            vmem(slots + ext, *tile),
             vmem(slots, *tile),
             pltpu.VMEM((24, LANES), jnp.int32),
             pltpu.SMEM((24, LANES), jnp.int32),

time: 34.3 us -> 33.3 us (0.971)
  Pallas kernels: 31.6 us -> 30.7 us
    pallas_call x1, Pallas kernels: 31.6 us -> 30.7 us  [local(): pl.pallas_call(make_kernel(outer, inner, count, face_dev, groups, nx, ny)...]
where the time goes in v4:
time: 33.3 us; the launch traced here: 33.2 us
  Pallas kernels  30.7 us (92%)
  local copies, waits for them, and re-layouts  1.84 us (6%)
  between operations  0.64 us (2%)
    pallas_call x1, Pallas kernels, local(): pl.pallas_call(make_kernel(outer, inner, count, face_dev, groups, nx, ny)...  30.7 us
    reshape x1, local copies, waits for them, and re-layouts, local(): return (sol.reshape(face_dev, width), res.reshape(face_dev, width))  1.84 us

profile of v4, /device:TPU:0, one launch (start us, length us, event | category | flops | bytes accessed | tf_op | source)
XLA Modules:
  0.0 33.2 jit_solution(3280317837006430823)
XLA Ops:
  0.6 30.7 %cg.1 = (f32[48,8,128]{2,1,0:T(8,128)}, f32[48,8,128]{2,1,0:T(8,128)}) custom-call(f32[48,1024]{1,0:T(8,128)} %heat_hbm.1, s32[6,16]{1,0:T(8,128)} %bitcast.9, f32[16,384,384]{2,1,0:T(8,128)} %stiff_ref.1), custom_call_target="tpu_custom_call" | custom-call | tf_op jit(solution)/shard_map/cg/pallas_call | solution.py:454
  31.3 1.8 %copy_bitcast_fusion = (f32[48,1024]{1,0:T(8,128)}, f32[48,1024]{1,0:T(8,128)}) fusion(f32[6,8,8,128]{3,2,1,0:T(8,128)} %bitcast.8, f32[6,8,8,128]{3,2,1,0:T(8,128)} %bitcast.7), kind=kLoop, calls=%fused_computation | loop fusion | bytes 786432 | tf_op jit(solution)/shard_map/reshape | solution.py:496
